TPU v7x, 512 devices: a whole 4x8x8 slice. The times are simulated.
512 devices in a mesh: ctx: 64 (over x, y, core), head: 8 (over z).
Axes of the slice: x: 4, y: 8, z: 8, core: 2. Of those that a mesh axis runs over, the one named last changes fastest.
Arguments:
- placement: int32 [64], replicated, may hold values from 0 to 63, each once
- placed_queries: bfloat16 [16384, 4096], P('ctx', 'head'), may hold values from -160 to 160
- placed_keys: bfloat16 [16384, 1024], P('ctx', 'head'), may hold values from -4.5 to 4.5
- placed_values: bfloat16 [16384, 1024], P('ctx', 'head'), may hold values from -6 to 6
- out_weight: bfloat16 [4096, 4096], P('head', 'ctx'), may hold values from -0.25 to 0.25
Outputs:
- attention_out: bfloat16 [16384, 4096], P('ctx', 'head')
Inputs may be any that keep to these rules, and one draw needn't show every extreme that they name: placement holds each of 0 .. 63 once.
All inputs are finite; a program needn't handle non-finite values.
Results may differ from a plain program's by a relative error of at most 0.015.
Values may be sent and summed in bfloat16 or wider, within the bound.
No kernel may reach another device: no remote copies, remote signals or barrier semaphores. Data moves between devices by JAX's collectives and lax.ppermute only.
A program may use at most 64 MiB of HBM per device.

v0:
```python
import jax
import jax.numpy as jnp
from jax import lax
from jax.sharding import PartitionSpec as P

HEAD_FEATURES = 128
masked_score = -1e30


def position_lookup(placement, device_ids):
    table = jnp.arange(placement.shape[0], dtype=jnp.int32)
    matches = device_ids[..., None] == table
    return jnp.sum(jnp.where(matches, placement, 0), axis=-1)


def attend(queries, positions, row_groups, placement, placed_keys, placed_values):
    total_rows = queries.shape[0]
    home_rows = placed_keys.shape[0]
    kv_heads = placed_keys.shape[1] // HEAD_FEATURES
    common_across = queries.shape[1] // placed_keys.shape[1]
    group_rows = total_rows // row_groups
    query_grid = queries.reshape(total_rows, kv_heads, common_across, HEAD_FEATURES)
    score_scale = HEAD_FEATURES ** (-0.5)
    initial = tuple(
        (
            (
                jnp.full((kv_heads, common_across, group_rows), masked_score, jnp.float32),
                jnp.zeros((kv_heads, common_across, group_rows), jnp.float32),
                jnp.zeros((kv_heads, common_across, group_rows, HEAD_FEATURES), jnp.float32),
            )
            for member in range(row_groups)
        )
    )

    def update(current, part_queries, part_positions, key_block, value_block, key_positions):
        running_max, running_sum, running_out = current
        scores = (
            jnp.einsum(
                "rkgd,skd->kgrs", part_queries, key_block, preferred_element_type=jnp.float32
            )
            * score_scale
        )
        allowed = key_positions[None, :] <= part_positions[:, None]
        scores = jnp.where(allowed, scores, masked_score)
        new_max = jnp.maximum(running_max, jnp.max(scores, axis=-1))
        weights = jnp.where(allowed, jnp.exp(scores - new_max[..., None]), 0.0)
        shrink = jnp.exp(running_max - new_max)
        new_sum = running_sum * shrink + jnp.sum(weights, axis=-1)
        new_out = running_out * shrink[..., None] + jnp.einsum(
            "kgrs,skd->kgrd",
            weights.astype(jnp.bfloat16),
            value_block,
            preferred_element_type=jnp.float32,
        )
        return (new_max, new_sum, new_out)

    key_piece = lax.all_gather(placed_keys, "ctx", axis=0, tiled=True)
    value_piece = lax.all_gather(placed_values, "ctx", axis=0, tiled=True)
    count = key_piece.shape[0]
    block_count = count // home_rows
    key_grid = key_piece.reshape(block_count, home_rows, kv_heads, HEAD_FEATURES)
    value_grid = value_piece.reshape(block_count, home_rows, kv_heads, HEAD_FEATURES)
    offsets = jnp.arange(block_count, dtype=jnp.int32) * home_rows

    def one_block(states, operands):
        key_block, value_block, block_first = operands
        key_index = block_first + jnp.arange(home_rows, dtype=jnp.int32)
        key_positions = (
            position_lookup(placement, key_index // home_rows) * home_rows + key_index % home_rows
        )
        earliest = jnp.min(key_positions)
        updated = [
            lax.cond(
                earliest <= jnp.max(positions),
                lambda current: update(
                    current, query_grid, positions, key_block, value_block, key_positions
                ),
                lambda current: current,
                states[0],
            )
        ]
        return (tuple(updated), None)

    finished, unused = lax.scan(one_block, initial, (key_grid, value_grid, offsets))
    outputs = [member_state[2] / member_state[1][..., None] for member_state in finished]
    joined = outputs[0]
    return (
        jnp.transpose(joined, (2, 0, 1, 3))
        .reshape(total_rows, queries.shape[1])
        .astype(jnp.bfloat16)
    )


def softmax_mixer(placement, placed_queries, placed_keys, placed_values):
    home_rows = placed_queries.shape[0]
    own_index = lax.axis_index("ctx")
    own_block = position_lookup(placement, own_index)
    positions = own_block * home_rows + jnp.arange(home_rows, dtype=jnp.int32)
    return attend(placed_queries, positions, 1, placement, placed_keys, placed_values)


def body(placement, placed_queries, placed_keys, placed_values, out_weight):
    hidden = softmax_mixer(placement, placed_queries, placed_keys, placed_values)
    partial_sum = jnp.dot(
        hidden,
        lax.all_gather(out_weight, "ctx", axis=1, tiled=True),
        preferred_element_type=jnp.float32,
    )
    rounded_term = lax.optimization_barrier(partial_sum.astype(jnp.bfloat16)).astype(jnp.float32)
    return lax.psum_scatter(
        rounded_term.astype(jnp.bfloat16), "head", scatter_dimension=1, tiled=True
    )


def solution(mesh):
    placed = (P(), P("ctx", "head"), P("ctx", "head"), P("ctx", "head"), P("head", "ctx"))
    return jax.shard_map(
        body, mesh=mesh, in_specs=placed, out_specs=P("ctx", "head"), check_vma=False
    )
```

profile of v0, /device:TPU:22, one launch (start us, length us, event | category | flops | bytes accessed | tf_op | source)
XLA Modules:
  0.0 729.8 jit_solution(3870190778058489720)
XLA Ops:
  12.7 84.4 %all-gather.4.cloned.1.call-done = bf16[16384,128]{1,0:T(8,128)(2,1)} async-done(((bf16[256,128]{1,0:T(8,128)(2,1)}), bf16[16384,128]{1,0:T(8,128)(2,1)}) %all-gather.4.cloned.1.call-update) | async-done | bytes 4194320 | tf_op jit(solution)/shard_map/all_gather | solution.py:57
  97.1 85.2 %all-gather.6.cloned.1.call-done = bf16[16384,128]{1,0:T(8,128)(2,1)} async-done(((bf16[256,128]{1,0:T(8,128)(2,1)}), bf16[16384,128]{1,0:T(8,128)(2,1)}) %all-gather.6.cloned.1.call-update) | async-done | bytes 4194320 | tf_op jit(solution)/shard_map/all_gather | solution.py:58
  182.4 474.6 %while.17 = (s32[]{:T(128)}, f32[1,4,256]{2,1,0:T(4,128)S(1)}, f32[1,4,256]{2,1,0:T(4,128)S(1)}, f32[1,4,256,128]{3,2,1,0:T(8,128)S(1)}, s32[64]{0:T(128)S(1)}, ...) while((s32[]{:T(128)}, f32[1,4,256]{2,1,0:T(4,128)S(1)}, ...), condition=%wide.region_9.10_spmd.clone, body=%wide.region_2.9_spmd.clone.sunk | while | flops 136964864 | bytes 4927015 | solution.py:84
  191.9 2.9 conditional.3
  199.6 2.9 conditional.3
  242.8 2.9 conditional.3
  301.4 2.9 conditional.3
  309.1 2.9 conditional.3
  337.0 2.9 conditional.3
  344.6 2.9 conditional.3
  352.3 2.9 conditional.3
  360.0 2.9 conditional.3
  367.7 2.9 conditional.3
  375.4 2.9 conditional.3
  383.1 2.9 conditional.3
  410.9 2.9 conditional.3
  418.6 2.9 conditional.3
  426.3 2.9 conditional.3
  434.0 2.9 conditional.3
  503.2 2.9 conditional.3
  510.9 2.9 conditional.3
  518.6 2.9 conditional.3
  657.3 4.8 convolution_convert_fusion
  662.1 61.2 %reduce-scatter.2.cloned.1.call-done = bf16[256,512]{1,0:T(8,128)(2,1)} async-done(((bf16[256,4096]{1,0:T(8,128)(2,1)}), bf16[256,512]{1,0:T(8,128)(2,1)}) %reduce-scatter.2.cloned.1.call-update) | async-done | bytes 262160 | tf_op jit(solution)/shard_map/reduce_scatter | solution.py:110
  (848 shorter events, 501.3 us)
Async XLA Ops:
  6.5 90.6 %all-gather.4.cloned.1.call-start = ((), (), s32[]{:S(2)}) async-start(), calls=%async_computation.1 | async-start | bytes 4259840 | tf_op jit(solution)/shard_map/all_gather | solution.py:57
  7.3 175.1 %all-gather.6.cloned.1.call-start = ((), (), s32[]{:S(2)}) async-start(), calls=%async_computation.2 | async-start | bytes 4259840 | tf_op jit(solution)/shard_map/all_gather | solution.py:58
  8.0 649.3 %all-gather.8.cloned.1.call-start = ((), (), s32[]{:S(2)}) async-start(), calls=%async_computation.3 | async-start | bytes 4259840 | tf_op jit(solution)/shard_map/all_gather | solution.py:106
  8.7 714.6 %reduce-scatter.2.cloned.1.call-start = ((), (), s32[]{:S(2)}) async-start(), calls=%async_computation.4 | async-start | bytes 2359296 | tf_op jit(solution)/shard_map/reduce_scatter | solution.py:110
Sparse Core Ops, SparseCore 0:
  10.7 86.3 all-gather.3
  100.5 81.7 all-gather.5
  185.7 82.0 all-gather.7
  662.2 61.0 reduce-scatter.1
where the time goes:
time: 739 us; the launch traced here: 730 us
  waiting for transfers between devices  233 us (32%)
  other arithmetic  196 us (27%)
  matrix products  151 us (20%)
  loops' own time  93.1 us (13%)
  local copies, waits for them, and re-layouts  43.4 us (6%)
  between operations  13.9 us (2%)
    another operation x1, loops' own time, attend(): lax.scan(one_block, initial, (key_grid, value_grid, offsets))  89.6 us
    reduce_min x64, other arithmetic, one_block(): earliest = jnp.min(key_positions)  85.5 us
    all_gather x1, waiting for transfers between devices, attend(): value_piece = lax.all_gather(placed_values, 'ctx', axis=0, tiled=True)  85.2 us
    all_gather x1, waiting for transfers between devices, attend(): key_piece = lax.all_gather(placed_keys, 'ctx', axis=0, tiled=True)  84.4 us
    dot_general x58, matrix products, update(): jnp.einsum('kgrs,skd->kgrd', weights.astype(jnp.bfloat16), value_block, p...  78.1 us
    dot_general x58, matrix products, update(): jnp.einsum('rkgd,skd->kgrs', part_queries, key_block, preferred_element_t...  67.8 us
    reduce_scatter x1, waiting for transfers between devices, body(): lax.psum_scatter(rounded_term.astype(jnp.bfloat16), 'head', scatter_dimen...  61.2 us
    reduce_sum x65, other arithmetic, position_lookup(): return jnp.sum(jnp.where(matches, placement, 0), axis=-1)  49.2 us
  transfers between devices with their start and end apart: 4, of which 3 were waited for; matrix products, arithmetic and copies ran while one was open for 53% of the time, Pallas kernels for 0%

commit v1 on v0

--- a/solution.py
+++ b/solution.py
@@ -54,7 +54,10 @@
         )
         return (new_max, new_sum, new_out)
 
-    key_piece = lax.all_gather(placed_keys, "ctx", axis=0, tiled=True)
+    devices = lax.axis_size("ctx")
+    pieces = jnp.stack([placed_keys for _ in range(devices)])
+    pieces = lax.all_to_all(pieces, "ctx", split_axis=0, concat_axis=0)
+    key_piece = jnp.concatenate(pieces, axis=0)
     value_piece = lax.all_gather(placed_values, "ctx", axis=0, tiled=True)
     count = key_piece.shape[0]
     block_count = count // home_rows

time: 739 us -> 640 us (0.87)
  the two profiles are of different devices: /device:TPU:22 before, /device:TPU:14 now
where the time goes in v1:
time: 640 us; the launch traced here: 631 us
  waiting for transfers between devices  176 us (28%)
  other arithmetic  149 us (23%)
  matrix products  144 us (22%)
  loops' own time  93 us (15%)
  local copies, waits for them, and re-layouts  44 us (7%)
  between operations  13.9 us (2%)
  starting transfers between devices  11.3 us (2%)
    all_to_all x1, waiting for transfers between devices, attend(): pieces = lax.all_to_all(pieces, 'ctx', split_axis=0, concat_axis=0)  103 us
    another operation x1, loops' own time, attend(): lax.scan(one_block, initial, (key_grid, value_grid, offsets))  89.6 us
    reduce_min x64, other arithmetic, one_block(): earliest = jnp.min(key_positions)  83.8 us
    dot_general x55, matrix products, update(): jnp.einsum('kgrs,skd->kgrd', weights.astype(jnp.bfloat16), value_block, p...  74.5 us
    reduce_scatter x1, waiting for transfers between devices, body(): lax.psum_scatter(rounded_term.astype(jnp.bfloat16), 'head', scatter_dimen...  71.6 us
    dot_general x55, matrix products, update(): jnp.einsum('rkgd,skd->kgrs', part_queries, key_block, preferred_element_t...  64.3 us
    dynamic_slice x64, local copies, waits for them, and re-layouts, attend(): lax.scan(one_block, initial, (key_grid, value_grid, offsets))  39.3 us
    select_n x64, other arithmetic, one_block(): key_index // home_rows  39.2 us
  transfers between devices with their start and end apart: 4, of which 2 were waited for; matrix products, arithmetic and copies ran while one was open for 53% of the time, Pallas kernels for 0%

profile of v1, /device:TPU:14, one launch (start us, length us, event | category | flops | bytes accessed | tf_op | source)
XLA Modules:
  0.0 631.1 jit_solution(12792474996413105700)
XLA Ops:
  7.3 3.8 stack.2
  11.1 11.2 %all-to-all-start = ((bf16[64,256,128]{2,1,0:T(8,128)(2,1)}), bf16[64,256,128]{2,1,0:T(8,128)(2,1)}, u32[]{:S(2)}, u32[]{:S(2)}) async-start(bf16[64,256,128]{2,1,0:T(8,128)(2,1)} %stack.2), calls=%async_computation | async-start | bytes 8388608 | tf_op jit(solution)/shard_map/all_to_all | solution.py:59
  25.4 102.9 %all-to-all-done = bf16[64,256,128]{2,1,0:T(8,128)(2,1)} async-done(((bf16[64,256,128]{2,1,0:T(8,128)(2,1)}), bf16[64,256,128]{2,1,0:T(8,128)(2,1)}, u32[]{:S(2)}, u32[]{:S(2)}) %all-to-all-start) | async-done | bytes 4194336 | tf_op jit(solution)/shard_map/all_to_all | solution.py:59
  128.4 419.4 %while.17 = (s32[]{:T(128)}, f32[1,4,256]{2,1,0:T(4,128)S(1)}, f32[1,4,256]{2,1,0:T(4,128)S(1)}, f32[1,4,256,128]{3,2,1,0:T(8,128)S(1)}, s32[64]{0:T(128)S(1)}, ...) while((s32[]{:T(128)}, f32[1,4,256]{2,1,0:T(4,128)S(1)}, ...), condition=%wide.region_9.10_spmd.clone, body=%wide.region_2.9_spmd.clone.sunk | while | flops 136964864 | bytes 4927015 | solution.py:87
  136.5 2.9 conditional.3
  143.5 2.9 conditional.3
  158.5 2.9 conditional.3
  165.5 2.9 conditional.3
  172.4 2.9 conditional.3
  211.3 2.9 conditional.3
  218.3 2.9 conditional.3
  282.1 2.9 conditional.3
  289.0 2.9 conditional.3
  348.8 2.9 conditional.3
  355.7 2.9 conditional.3
  383.6 2.9 conditional.3
  390.5 2.9 conditional.3
  418.4 2.9 conditional.3
  425.4 2.9 conditional.3
  453.2 2.9 conditional.3
  460.2 2.9 conditional.3
  530.9 2.9 conditional.3
  548.1 4.8 convolution_convert_fusion
  552.9 71.6 %reduce-scatter.2.cloned.1.call-done = bf16[256,512]{1,0:T(8,128)(2,1)} async-done(((bf16[256,4096]{1,0:T(8,128)(2,1)}), bf16[256,512]{1,0:T(8,128)(2,1)}) %reduce-scatter.2.cloned.1.call-update) | async-done | bytes 262160 | tf_op jit(solution)/shard_map/reduce_scatter | solution.py:113
  (828 shorter events, 438.4 us)
Async XLA Ops:
  6.5 121.8 %all-gather.3.cloned.1.call-start = ((), (), s32[]{:S(2)}) async-start(), calls=%async_computation.2 | async-start | bytes 4259840 | tf_op jit(solution)/shard_map/all_gather | solution.py:61
  11.1 12.0 %copy-start.1 = (s32[64]{0:T(128)S(1)}, s32[64]{0:T(128)}, u32[]{:S(2)}) copy-start(s32[64]{0:T(128)} %param.9) | copy-start | bytes 772
  11.1 14.0 %copy-start = (bf16[256,512]{1,0:T(8,128)(2,1)S(1)}, bf16[256,512]{1,0:T(8,128)(2,1)}, u32[]{:S(2)}) copy-start(bf16[256,512]{1,0:T(8,128)(2,1)} %param.10) | copy-start | bytes 786436
  11.1 117.3 %all-to-all-start = ((bf16[64,256,128]{2,1,0:T(8,128)(2,1)}), bf16[64,256,128]{2,1,0:T(8,128)(2,1)}, u32[]{:S(2)}, u32[]{:S(2)}) async-start(bf16[64,256,128]{2,1,0:T(8,128)(2,1)} %stack.2), calls=%async_computation | async-start | bytes 8388608 | tf_op jit(solution)/shard_map/all_to_all | solution.py:59
  22.3 525.8 %all-gather.5.cloned.1.call-start = ((), (), s32[]{:S(2)}) async-start(), calls=%async_computation.3 | async-start | bytes 4259840 | tf_op jit(solution)/shard_map/all_gather | solution.py:109
  23.0 601.5 %reduce-scatter.2.cloned.1.call-start = ((), (), s32[]{:S(2)}) async-start(), calls=%async_computation.4 | async-start | bytes 2359296 | tf_op jit(solution)/shard_map/reduce_scatter | solution.py:113
Sparse Core Ops, SparseCore 0:
  10.7 102.3 all-gather.2
  116.5 82.7 all-gather.4
  553.1 71.4 reduce-scatter.1
